TPU v7x, 32 devices: a whole 2x2x4 slice. The times are simulated.
32 devices in a mesh: groups: 2 (over x), seq: 8 (over z, y), chan: 2 (over core).
Axes of the slice: x: 2, y: 2, z: 4, core: 2. Of those that a mesh axis runs over, the one named last changes fastest.
Arguments:
- stream: bfloat16 [4096, 2048], P(('groups', 'seq'), 'chan'), parts along dimension 0, may hold values from -6 to 6
- nucleotide_token_ids: int32 [4096], P(('groups', 'seq')), parts along dimension 0, may hold values from 4 to 11, as said below
- genome_length: int32 [2], P('groups'), parts along dimension 0, may hold values from 1024 to 2048
- embedding: bfloat16 [16, 2048], replicated, may hold values from -6 to 6
- attention_in: bfloat16 [2048, 3, 1024], P(None, None, 'chan'), may hold values from -0.125 to 0.125
- scan_input: bfloat16 [2048, 1024], P(None, 'chan'), may hold values from -0.125 to 0.125
- state_maps: bfloat16 [2048, 256], P(None, 'chan'), may hold values from -0.125 to 0.125
- step_weight: bfloat16 [2048, 8], P(None, 'chan'), may hold values from -0.125 to 0.125
- step_bias: float32 [8], P('chan'), may hold values from -1 to 1
- head_decay_speed: float32 [8], P('chan'), as said below
- attention_gain: float32 [1024], P('chan'), may hold values from 0.25 to 1.75
- scan_gain: float32 [1024], P('chan'), may hold values from 0.25 to 1.75
- out_weight: bfloat16 [1024, 2048], P('chan'), may hold values from -0.1875 to 0.1875
Outputs:
- block_out: bfloat16 [4096, 2048], P(('groups', 'seq'), 'chan'), parts along dimension 0
There are 2 independent parts, one for each index of `groups`. A program takes and returns all parts, laid end to end along the dimension named above; an argument that names none is the same for every part. Nothing has to cross between parts.
Inputs may be any that keep to these rules, and one draw needn't show every extreme that they name: `nucleotide_token_ids`: positions below genome_length hold bases 7 to 10, except exactly three positions that hold 11, one in each third of the valid range; positions at or above genome_length hold 4. `head_decay_speed`: every entry lies between 1 / 20480 and 8 / 256.
All inputs are finite; a program needn't handle non-finite values.
Results may differ from a plain program's by a relative error of at most 0.0058.
Values may be sent and summed in bfloat16 or wider, within the bound.
A program may use at most 128 MiB of HBM per device.

v0:
```python
import math
import jax
import jax.numpy as jnp
from jax import lax
from jax.sharding import PartitionSpec as P

HEAD_DIM = 128
STATE = 64
epsilon_norm = 1e-06
spike_logarithm = math.log(0.7)
unclear_nucleotide = 11


def passed_along(block, axis, distance):
    devices = range(lax.axis_size(axis))
    route = [((i - distance) % len(devices), i) for i in devices]
    return lax.ppermute(block, axis, route)


def normalize(values):
    return values * lax.rsqrt(jnp.mean(values * values, axis=-1, keepdims=True) + epsilon_norm)


def compose(earlier_part, later_part):
    return (
        earlier_part[0] * later_part[0],
        later_part[0][:, None, None] * earlier_part[1] + later_part[1],
    )


def key_block(query_tile_rows, key_fragment, value_piece, key_position, valid_limit, score_scale):
    scores = (
        jnp.einsum(
            "epq,fpq->pef", query_tile_rows, key_fragment, preferred_element_type=jnp.float32
        )
        * score_scale
    )
    weights = jnp.where((key_position < valid_limit)[None, None, :], jnp.exp(scores), 0.0)
    totals = jnp.sum(weights, axis=-1).T
    numerator = jnp.einsum(
        "gfa,agn->fgn",
        weights.astype(jnp.bfloat16),
        value_piece,
        preferred_element_type=jnp.float32,
    )
    return (numerator, totals)


def local(
    stream,
    nucleotide_token_ids,
    genome_length,
    embedding,
    attention_in,
    scan_input,
    state_maps,
    step_weight,
    step_bias,
    head_decay_speed,
    attention_gain,
    scan_gain,
    out_weight,
):
    row_count = stream.shape[0]
    model_width = embedding.shape[1]
    head_count = step_weight.shape[1]
    score_scale = 2.0 / math.sqrt(HEAD_DIM)
    valid_limit = genome_length[0]
    position = lax.axis_index("seq") * row_count + jnp.arange(row_count, dtype=jnp.int32)
    key_valid = position < valid_limit
    gathered = lax.all_gather(stream, "chan", axis=1, tiled=True)
    onehot = (
        nucleotide_token_ids[:, None] == jnp.arange(embedding.shape[0], dtype=jnp.int32)[None, :]
    ).astype(jnp.bfloat16)
    hidden = (
        gathered.astype(jnp.float32)
        + jnp.dot(onehot, embedding, preferred_element_type=jnp.float32)
    ).astype(jnp.bfloat16)
    projected = jnp.dot(
        hidden,
        attention_in.reshape(model_width, 3 * head_count * HEAD_DIM),
        preferred_element_type=jnp.float32,
    ).reshape(row_count, 3, head_count, HEAD_DIM)
    queries = normalize(projected[:, 0]).astype(jnp.bfloat16)
    keyset = normalize(projected[:, 1]).astype(jnp.bfloat16)
    valueset = projected[:, 2].astype(jnp.bfloat16)
    empty_numer = jnp.zeros((row_count, head_count, HEAD_DIM), jnp.float32)
    empty_total = jnp.zeros((row_count, head_count), jnp.float32)
    carry_pair = (empty_numer, empty_total)
    key_fragment = lax.all_gather(keyset, "seq", axis=0, tiled=True)
    value_piece = lax.all_gather(valueset, "seq", axis=0, tiled=True)
    piece_rows = key_fragment.shape[0]
    block_count = piece_rows // 512

    def absorb_block(running, element):
        key_block_rows, value_block_rows, first_row = element
        numer_part, total_part = key_block(
            queries,
            key_block_rows,
            value_block_rows,
            first_row + jnp.arange(512, dtype=jnp.int32),
            valid_limit,
            score_scale,
        )
        return ((running[0] + numer_part, running[1] + total_part), None)

    first_rows = 512 * jnp.arange(block_count, dtype=jnp.int32)
    carry_pair, _ = lax.scan(
        absorb_block,
        carry_pair,
        (
            key_fragment.reshape(block_count, 512, head_count, HEAD_DIM),
            value_piece.reshape(block_count, 512, head_count, HEAD_DIM),
            first_rows,
        ),
    )
    numerator, totals = carry_pair
    attended = normalize(numerator / totals[:, :, None])
    inputs = (
        jax.nn.silu(jnp.dot(hidden, scan_input, preferred_element_type=jnp.float32))
        .astype(jnp.bfloat16)
        .reshape(row_count, head_count, HEAD_DIM)
    )
    state_rows = jax.nn.silu(
        jnp.dot(hidden, state_maps, preferred_element_type=jnp.float32)
    ).astype(jnp.bfloat16)
    input_map = state_rows[:, :STATE]
    output_map = state_rows[:, STATE:]
    step_list = jax.nn.softplus(
        jnp.dot(hidden, step_weight, preferred_element_type=jnp.float32) + step_bias[None, :]
    )
    usable_rows = key_valid.astype(jnp.float32)[:, None]
    spike_events = jnp.where(nucleotide_token_ids == unclear_nucleotide, spike_logarithm, 0.0)[
        :, None
    ]
    logarithm_decay = usable_rows * (-head_decay_speed[None, :] * step_list + spike_events)
    used_steps = usable_rows * step_list
    forward = jnp.cumsum(logarithm_decay, axis=0)
    backward = jnp.flip(jnp.cumsum(jnp.flip(logarithm_decay, 0), axis=0), 0)
    inputs_wide = inputs.astype(jnp.float32)
    scaled_forward = (
        (jnp.exp(forward[-1:] - forward) * used_steps)[:, :, None] * inputs_wide
    ).astype(jnp.bfloat16)
    scaled_backward = (
        (jnp.exp(backward[:1] - backward) * used_steps)[:, :, None] * inputs_wide
    ).astype(jnp.bfloat16)
    own_forward = (
        jnp.exp(forward[-1]),
        jnp.einsum("the,ts->hes", scaled_forward, input_map, preferred_element_type=jnp.float32),
    )
    own_backward = (
        jnp.exp(backward[0]),
        jnp.einsum("the,ts->hes", scaled_backward, input_map, preferred_element_type=jnp.float32),
    )
    section_count = lax.axis_size("seq").bit_length() - 1
    distances = [1] + [1 << section for section in range(section_count)]
    window_forward = own_forward
    window_backward = own_backward
    for section_index, distance in enumerate(distances):
        received_up = passed_along((window_forward[0], window_forward[1]), "seq", distance)
        received_down = passed_along((window_backward[0], window_backward[1]), "seq", -distance)
        if section_index == 0:
            window_forward = received_up
            window_backward = received_down
        else:
            window_forward = compose(received_up, window_forward)
            window_backward = compose(received_down, window_backward)
    enter_forward = window_forward[1] / (1.0 - window_forward[0])[:, None, None]
    enter_backward = window_backward[1] / (1.0 - window_backward[0])[:, None, None]
    pairing = jnp.dot(output_map, input_map.T, preferred_element_type=jnp.float32)
    block_rows = jnp.arange(row_count)
    causal_mask = block_rows[:, None] >= block_rows[None, :]
    read_wide = output_map.astype(jnp.float32)

    def strand(cumulative, allowed, entering):
        across = cumulative.T
        exponent = across[:, :, None] - across[:, None, :]
        mixing = (
            pairing[None]
            * jnp.exp(jnp.where(allowed[None], exponent, -jnp.inf))
            * used_steps.T[:, None, :]
        ).astype(jnp.bfloat16)
        local_part = jnp.einsum("htu,uhe->the", mixing, inputs, preferred_element_type=jnp.float32)
        carried = jnp.exp(cumulative)[:, :, None] * jnp.einsum(
            "ts,hes->the", read_wide, entering, precision=lax.Precision.HIGHEST
        )
        return local_part + carried

    scanned = normalize(
        strand(forward, causal_mask, enter_forward)
        + strand(backward, causal_mask.T, enter_backward)
    )
    combined = (
        (
            attention_gain.reshape(head_count, HEAD_DIM) * attended
            + scan_gain.reshape(head_count, HEAD_DIM) * scanned
        )
        .astype(jnp.bfloat16)
        .reshape(row_count, head_count * HEAD_DIM)
    )
    partial_out = jnp.dot(combined, out_weight, preferred_element_type=jnp.float32)
    summed = lax.psum_scatter(partial_out, "chan", scatter_dimension=1, tiled=True)
    return (stream.astype(jnp.float32) + summed).astype(jnp.bfloat16)


def solution(mesh):
    placed = (
        P(("groups", "seq"), "chan"),
        P(("groups", "seq")),
        P("groups"),
        P(),
        P(None, None, "chan"),
        P(None, "chan"),
        P(None, "chan"),
        P(None, "chan"),
        P("chan"),
        P("chan"),
        P("chan"),
        P("chan"),
        P("chan", None),
    )
    return jax.shard_map(
        local, mesh=mesh, in_specs=placed, out_specs=P(("groups", "seq"), "chan"), check_vma=False
    )
```

profile of v0, /device:TPU:0, one launch (start us, length us, event | category | flops | bytes accessed | tf_op | source)
XLA Modules:
  0.0 197.7 jit_solution(5060600774243856370)
XLA Ops:
  7.3 8.9 %copy.26 = bf16[2048,3,512]{0,2,1:T(8,128)(2,1)} copy(bf16[2048,3,512]{2,0,1:T(8,128)(2,1)} %param.19) | data formatting | bytes 12582912 | tf_op args[4]
  16.2 4.4 %all-gather.5.cloned.1.call-done = bf16[256,2048]{1,0:T(8,128)(2,1)} async-done(((bf16[256,1024]{1,0:T(8,128)(2,1)}), bf16[256,2048]{1,0:T(8,128)(2,1)}) %all-gather.5.cloned.1.call-update) | async-done | bytes 1048592 | tf_op jit(solution)/shard_map/all_gather | solution.py:71
  20.7 1.7 fusion.13
  22.4 5.0 %fusion.17 = f32[256,3,4,128]{0,3,2,1:T(8,128)S(1)} fusion(bf16[3,4,128,2048]{3,2,1,0:T(8,128)(2,1)} %bitcast.158, bf16[256,2048]{1,0:T(8,128)(2,1)S(1)} %fusion.13), kind=kOutput, calls=%fused_computation.29 | convolution fusion | flops 1610612736 | bytes 8912896 | tf_op jit(solution)/shard_map/dot_general | solution.py:79
  31.5 1.8 slice.90
  33.2 2.2 %add_multiply_fusion.1 = (f32[4,256]{1,0:T(4,128)S(1)}, f32[4,256]{1,0:T(4,128)}, f32[256,4]{0,1:T(4,128)S(1)}) fusion(f32[256]{0:T(256)S(1)} %compare_select_fusion.2, f32[4]{0:T(128)S(1)} %neg.22, f32[256]{0:T(256)S(1)} %compare_convert_fusion, f32[4]{0:T(128)S(1)} %copy-done.11, bf16[256,2048]{1,0:T(8,128)(2,1)} %copy-done.3, ...), kind=kOutput, calls=%fused_computation.121 | convolution fusion | flops 4205568 | bytes 1079328 | tf_op jit(solution)/shard_map/dot_general | solution.py:130
  37.8 1.7 collective-permute-start
  39.6 1.9 multiply_convert_fusion.7
  41.5 2.7 %fusion.43 = bf16[32,4,8,128]{3,2,1,0:T(8,128)(2,1)S(1)} fusion(bf16[256,2048]{1,0:T(8,128)(2,1)} %copy-done.3, bf16[2048,512]{1,0:T(8,128)(2,1)} %param.20), kind=kOutput, calls=%fused_computation.72 | convolution fusion | flops 537526272 | bytes 3407872 | tf_op jit(solution)/shard_map/dot_general | solution.py:120
  45.2 1.5 collective-permute-start.3
  49.5 3.2 %collective-permute-start.8 = (f32[4]{0:T(128)}, f32[4]{0:T(128)}, u32[]{:S(2)}, u32[]{:S(2)}) collective-permute-start(f32[4]{0:T(128)} %exp.54), channel_id=1, source_target_pairs={{2,0},{4,2},{6,4},{8,6},{10,8},{12,10},{14,12},{0,14},{3,1},{5,3},... | collective-permute-start | bytes 56 | tf_op jit(solution)/shard_map/ppermute | solution.py:17
  54.6 1.5 convolution_bitcast_fusion.2
  56.6 1.7 collective-permute-start.1
  58.4 3.0 %collective-permute-start.9 = (f32[4]{0:T(128)}, f32[4]{0:T(128)S(1)}, u32[]{:S(2)}, u32[]{:S(2)}) collective-permute-start(f32[4]{0:T(128)} %collective-permute-done.8), channel_id=1, source_target_pairs={{2,0},{4,2},{6,4},{8,6},{10,8},{12,10},{14,12},{0,14},{3,1},{5,3},... | collective-permute-start | bytes 56 | tf_op jit(solution)/shard_map/ppermute | solution.py:17
  61.4 1.7 collective-permute-done.1
  64.4 3.8 %collective-permute-start.10 = (f32[4]{0:T(128)S(1)}, f32[4]{0:T(128)S(1)}, u32[]{:S(2)}, u32[]{:S(2)}) collective-permute-start(f32[4]{0:T(128)S(1)} %mul.298), channel_id=1, source_target_pairs={{4,0},{6,2},{8,4},{10,6},{12,8},{14,10},{0,12},{2,14},{5,1},{7,3},... | collective-permute-start | bytes 56 | tf_op jit(solution)/shard_map/ppermute | solution.py:17
  69.5 2.5 %collective-permute-start.15 = (f32[4]{0:T(128)S(1)}, f32[4]{0:T(128)S(1)}, u32[]{:S(2)}, u32[]{:S(2)}) collective-permute-start(f32[4]{0:T(128)S(1)} %mul.299), channel_id=1, source_target_pairs={{8,0},{10,2},{12,4},{14,6},{0,8},{2,10},{4,12},{6,14},{9,1},{11,3}... | collective-permute-start | bytes 56 | tf_op jit(solution)/shard_map/ppermute | solution.py:17
  72.0 1.5 collective-permute-done.7
  74.0 1.7 collective-permute-start.4
  75.7 3.8 %collective-permute-done.12 = f32[4,128,64]{1,2,0:T(8,128)S(1)} collective-permute-done((f32[4,128,64]{1,2,0:T(8,128)S(1)}, f32[4,128,64]{1,2,0:T(8,128)S(1)}, u32[]{:S(2)}, u32[]{:S(2)}) %collective-permute-start.12) | collective-permute-done | bytes 131104 | tf_op jit(solution)/shard_map/ppermute | solution.py:17
  80.2 1.9 collective-permute-start.13
  82.1 3.3 %collective-permute-done.4 = f32[4,128,64]{1,2,0:T(8,128)S(1)} collective-permute-done((f32[4,128,64]{1,2,0:T(8,128)S(1)}, f32[4,128,64]{1,2,0:T(8,128)S(1)}, u32[]{:S(2)}, u32[]{:S(2)}) %collective-permute-start.4) | collective-permute-done | bytes 131104 | tf_op jit(solution)/shard_map/ppermute | solution.py:17
  86.7 7.5 %collective-permute-start.14 = (f32[4,128,64]{1,2,0:T(8,128)S(1)}, f32[4,128,64]{1,2,0:T(8,128)S(1)}, u32[]{:S(2)}, u32[]{:S(2)}) collective-permute-start(f32[4,128,64]{1,2,0:T(8,128)S(1)} %multiply_add_fusion), channel_id=1, source_target_pairs={{8,0},{10,2},{12,4},{14,6},{0,8},{2,10},{4,12},{6,14},{9,1},{11,3}... | collective-permute-start | bytes 393224 | tf_op jit(solution)/shard_map/ppermute | solution.py:17
  94.2 3.7 %collective-permute-done.5 = f32[4,128,64]{1,2,0:T(8,128)S(1)} collective-permute-done((f32[4,128,64]{1,2,0:T(8,128)S(1)}, f32[4,128,64]{1,2,0:T(8,128)S(1)}, u32[]{:S(2)}, u32[]{:S(2)}) %collective-permute-start.5) | collective-permute-done | bytes 131104 | tf_op jit(solution)/shard_map/ppermute | solution.py:17
  98.0 1.3 collective-permute-start.6
  99.3 2.2 %collective-permute-done.14 = f32[4,128,64]{1,2,0:T(8,128)S(1)} collective-permute-done((f32[4,128,64]{1,2,0:T(8,128)S(1)}, f32[4,128,64]{1,2,0:T(8,128)S(1)}, u32[]{:S(2)}, u32[]{:S(2)}) %collective-permute-start.14) | collective-permute-done | bytes 131104 | tf_op jit(solution)/shard_map/ppermute | solution.py:17
  102.0 6.3 %collective-permute-done.6 = f32[4,128,64]{1,2,0:T(8,128)S(1)} collective-permute-done((f32[4,128,64]{1,2,0:T(8,128)S(1)}, f32[4,128,64]{1,2,0:T(8,128)S(1)}, u32[]{:S(2)}, u32[]{:S(2)}) %collective-permute-start.6) | collective-permute-done | bytes 131104 | tf_op jit(solution)/shard_map/ppermute | solution.py:17
  108.8 4.5 %reshape.152 = bf16[4,512,4,128]{1,0,3,2:T(4,128)(2,1)} reshape(bf16[2048,4,128]{0,2,1:T(8,128)(2,1)} %all-gather.7.cloned.1.call-done) | data formatting | bytes 4194304 | tf_op jit(solution)/shard_map/reshape | solution.py:112
  113.3 4.5 %copy.28 = bf16[4,512,4,128]{3,1,2,0:T(8,128)(2,1)} copy(bf16[4,512,4,128]{1,0,3,2:T(4,128)(2,1)} %reshape.152) | data formatting | bytes 4194304
  117.8 24.4 %all-gather.9.cloned.1.call-done = bf16[2048,1,4,128]{0,3,2,1:T(8,128)(2,1)} async-done(((bf16[256,1,4,128]{0,3,2,1:T(8,128)(2,1)}), bf16[2048,1,4,128]{0,3,2,1:T(8,128)(2,1)}) %all-gather.9.cloned.1.call-update) | async-done | bytes 2097168 | tf_op jit(solution)/shard_map/all_gather | solution.py:91
  142.3 4.5 %reshape.151 = bf16[4,512,4,128]{1,0,3,2:T(4,128)(2,1)} reshape(bf16[2048,1,4,128]{0,3,2,1:T(8,128)(2,1)} %all-gather.9.cloned.1.call-done) | data formatting | bytes 4194304 | tf_op jit(solution)/shard_map/reshape | solution.py:113
  146.8 3.4 %copy.27 = bf16[4,512,4,128]{1,3,2,0:T(8,128)(2,1)} copy(bf16[4,512,4,128]{1,0,3,2:T(4,128)(2,1)} %reshape.151) | data formatting | bytes 4194304
  150.1 28.5 %while.13 = (s32[]{:T(128)}, f32[256,4,128]{0,2,1:T(8,128)S(1)}, f32[256,4]{0,1:T(4,128)S(1)}, bf16[4,512,4,128]{1,3,2,0:T(8,128)(2,1)}, s32[4]{0:T(128)S(1)}, /...) while((s32[]{:T(128)}, f32[256,4,128]{0,2,1:T(8,128)S(1)}, ...), condition=%wide.region_4.5_spmd.clone, body=%wide.region_2.4_spmd.clone.sunk | while | flops 271845376 | bytes 6572676 | solution.py:108
  150.7 1.3 add_compare_fusion.2
  152.0 2.9 %bitcast_reduce_fusion.2 = (f32[4,256]{1,0:T(4,128)S(1)}, f32[4,512,256]{2,1,0:T(8,128)}) fusion(pred[512]{0:T(512)(128)(4,1)S(1)} %add_compare_fusion.2, bf16[256,4,128]{2,0,1:T(8,128)(2,1)S(1)} %get-tuple-element.209, bf16[4,512,4,128]{3,1,2,0:T(8,128)(2,1)} %get-tuple-element.208, s32[]{:T(128)} %get-tuple-element.192), kind=kOutput, calls=%fused_computation.clone.1 | convolution fusion | flops 135789568 | bytes 2888704 | tf_op jit(solution)/shard_map/while/body/eval_jaxpr/epq,fpq->pef/dot_general | solution.py:33
  154.9 2.3 %fusion.94 = f32[256,4,128]{0,2,1:T(8,128)S(1)} fusion(f32[4,512,256]{2,1,0:T(8,128)} %get-tuple-element.180, pred[512]{0:T(512)(128)(4,1)S(1)} %add_compare_fusion.2, f32[256,4,128]{0,2,1:T(8,128)S(1)} %get-tuple-element.193, bf16[4,512,4,128]{1,3,2,0:T(8,128)(2,1)} %get-tuple-element.205, s32[]{:T(128)} %get-tuple-element.192, pred[]{:T(512)S(6)} %compare.3), kind=kOutput, calls=%fused_computation.4.clone.1 | convolution fusion | flops 136052736 | bytes 3671041 | tf_op jit(solution)/shard_map/while/body/eval_jaxpr/gfa,agn->fgn/dot_general | solution.py:40
  157.9 1.3 add_compare_fusion.2
  159.2 2.9 %bitcast_reduce_fusion.2 = (f32[4,256]{1,0:T(4,128)S(1)}, f32[4,512,256]{2,1,0:T(8,128)}) fusion(pred[512]{0:T(512)(128)(4,1)S(1)} %add_compare_fusion.2, bf16[256,4,128]{2,0,1:T(8,128)(2,1)S(1)} %get-tuple-element.209, bf16[4,512,4,128]{3,1,2,0:T(8,128)(2,1)} %get-tuple-element.208, s32[]{:T(128)} %get-tuple-element.192), kind=kOutput, calls=%fused_computation.clone.1 | convolution fusion | flops 135789568 | bytes 2888704 | tf_op jit(solution)/shard_map/while/body/eval_jaxpr/epq,fpq->pef/dot_general | solution.py:33
  162.1 2.3 %fusion.94 = f32[256,4,128]{0,2,1:T(8,128)S(1)} fusion(f32[4,512,256]{2,1,0:T(8,128)} %get-tuple-element.180, pred[512]{0:T(512)(128)(4,1)S(1)} %add_compare_fusion.2, f32[256,4,128]{0,2,1:T(8,128)S(1)} %get-tuple-element.193, bf16[4,512,4,128]{1,3,2,0:T(8,128)(2,1)} %get-tuple-element.205, s32[]{:T(128)} %get-tuple-element.192, pred[]{:T(512)S(6)} %compare.3), kind=kOutput, calls=%fused_computation.4.clone.1 | convolution fusion | flops 136052736 | bytes 3671041 | tf_op jit(solution)/shard_map/while/body/eval_jaxpr/gfa,agn->fgn/dot_general | solution.py:40
  165.0 1.3 add_compare_fusion.2
  166.3 2.9 %bitcast_reduce_fusion.2 = (f32[4,256]{1,0:T(4,128)S(1)}, f32[4,512,256]{2,1,0:T(8,128)}) fusion(pred[512]{0:T(512)(128)(4,1)S(1)} %add_compare_fusion.2, bf16[256,4,128]{2,0,1:T(8,128)(2,1)S(1)} %get-tuple-element.209, bf16[4,512,4,128]{3,1,2,0:T(8,128)(2,1)} %get-tuple-element.208, s32[]{:T(128)} %get-tuple-element.192), kind=kOutput, calls=%fused_computation.clone.1 | convolution fusion | flops 135789568 | bytes 2888704 | tf_op jit(solution)/shard_map/while/body/eval_jaxpr/epq,fpq->pef/dot_general | solution.py:33
  169.2 2.3 %fusion.94 = f32[256,4,128]{0,2,1:T(8,128)S(1)} fusion(f32[4,512,256]{2,1,0:T(8,128)} %get-tuple-element.180, pred[512]{0:T(512)(128)(4,1)S(1)} %add_compare_fusion.2, f32[256,4,128]{0,2,1:T(8,128)S(1)} %get-tuple-element.193, bf16[4,512,4,128]{1,3,2,0:T(8,128)(2,1)} %get-tuple-element.205, s32[]{:T(128)} %get-tuple-element.192, pred[]{:T(512)S(6)} %compare.3), kind=kOutput, calls=%fused_computation.4.clone.1 | convolution fusion | flops 136052736 | bytes 3671041 | tf_op jit(solution)/shard_map/while/body/eval_jaxpr/gfa,agn->fgn/dot_general | solution.py:40
  172.1 1.3 add_compare_fusion.2
  173.4 2.9 %bitcast_reduce_fusion.2 = (f32[4,256]{1,0:T(4,128)S(1)}, f32[4,512,256]{2,1,0:T(8,128)}) fusion(pred[512]{0:T(512)(128)(4,1)S(1)} %add_compare_fusion.2, bf16[256,4,128]{2,0,1:T(8,128)(2,1)S(1)} %get-tuple-element.209, bf16[4,512,4,128]{3,1,2,0:T(8,128)(2,1)} %get-tuple-element.208, s32[]{:T(128)} %get-tuple-element.192), kind=kOutput, calls=%fused_computation.clone.1 | convolution fusion | flops 135789568 | bytes 2888704 | tf_op jit(solution)/shard_map/while/body/eval_jaxpr/epq,fpq->pef/dot_general | solution.py:33
  176.3 2.3 %fusion.94 = f32[256,4,128]{0,2,1:T(8,128)S(1)} fusion(f32[4,512,256]{2,1,0:T(8,128)} %get-tuple-element.180, pred[512]{0:T(512)(128)(4,1)S(1)} %add_compare_fusion.2, f32[256,4,128]{0,2,1:T(8,128)S(1)} %get-tuple-element.193, bf16[4,512,4,128]{1,3,2,0:T(8,128)(2,1)} %get-tuple-element.205, s32[]{:T(128)} %get-tuple-element.192, pred[]{:T(512)S(6)} %compare.3), kind=kOutput, calls=%fused_computation.4.clone.1 | convolution fusion | flops 136052736 | bytes 3671041 | tf_op jit(solution)/shard_map/while/body/eval_jaxpr/gfa,agn->fgn/dot_general | solution.py:40
  179.0 2.1 %fusion.77 = f32[256,2048]{1,0:T(8,128)} fusion(bf16[256,512]{0,1:T(8,128)(2,1)S(1)} %bitcast.159, bf16[512,2048]{1,0:T(8,128)(2,1)S(1)} %copy-done), kind=kOutput, calls=%fused_computation.137 | convolution fusion | flops 536870912 | bytes 4456448 | tf_op jit(solution)/shard_map/dot_general | solution.py:201
  181.1 7.9 %reduce-scatter.2.cloned.1.call-done = f32[256,1024]{1,0:T(8,128)} async-done(((f32[256,2048]{1,0:T(8,128)}), f32[256,1024]{1,0:T(8,128)}) %reduce-scatter.2.cloned.1.call-update) | async-done | bytes 1048592 | tf_op jit(solution)/shard_map/reduce_scatter | solution.py:202
  189.0 2.2 %add_convert_fusion = bf16[256,1024]{1,0:T(8,128)(2,1)} fusion(f32[256,1024]{1,0:T(8,128)} %reduce-scatter.2.cloned.1.call-done, bf16[256,1024]{1,0:T(8,128)(2,1)S(1)} %copy-done.2), kind=kLoop, calls=%fused_computation.31 | loop fusion | flops 786432 | bytes 2097152 | tf_op jit(solution)/shard_map/convert_element_type | solution.py:203
  (121 shorter events, 21.5 us)
Async XLA Ops:
  6.5 172.5 %copy-start = (bf16[512,2048]{1,0:T(8,128)(2,1)S(1)}, bf16[512,2048]{1,0:T(8,128)(2,1)}, u32[]{:S(2)}) copy-start(bf16[512,2048]{1,0:T(8,128)(2,1)} %param.27) | copy-start | bytes 6291460
  6.5 14.1 %all-gather.5.cloned.1.call-start = ((), (), s32[]{:S(2)}) async-start(), calls=%async_computation.1 | async-start | bytes 1572864 | tf_op jit(solution)/shard_map/all_gather | solution.py:71
  7.3 13.4 %copy-start.4 = (bf16[16,2048]{1,0:T(8,128)(2,1)S(1)}, bf16[16,2048]{1,0:T(8,128)(2,1)}, u32[]{:S(2)}) copy-start(bf16[16,2048]{1,0:T(8,128)(2,1)} %param.18) | copy-start | bytes 196612
  7.3 13.4 %copy-start.6 = (s32[256]{0:T(256)S(1)}, s32[256]{0:T(256)}, u32[]{:S(2)}) copy-start(s32[256]{0:T(256)} %param.16) | copy-start | bytes 3076
  7.3 101.5 %all-gather.7.cloned.1.call-start = ((), (), s32[]{:S(2)}) async-start(), calls=%async_computation.2 | async-start | bytes 2359296 | tf_op jit(solution)/shard_map/all_gather | solution.py:90
  22.4 5.1 %copy-start.3 = (bf16[256,2048]{1,0:T(8,128)(2,1)}, bf16[256,2048]{1,0:T(8,128)(2,1)S(1)}, u32[]{:S(2)}) copy-start(bf16[256,2048]{1,0:T(8,128)(2,1)S(1)} %fusion.13) | copy-start | bytes 3145732
  27.5 1.2 copy-start.1
  27.5 2.7 %copy-start.10 = (f32[4]{0:T(128)S(1)}, f32[4]{0:T(128)}, u32[]{:S(2)}) copy-start(f32[4]{0:T(128)} %param.24) | copy-start | bytes 52
  27.5 5.7 %copy-start.9 = (bf16[2048,4]{0,1:T(4,128)(2,1)S(1)}, bf16[2048,4]{0,1:T(4,128)(2,1)}, u32[]{:S(2)}) copy-start(bf16[2048,4]{0,1:T(4,128)(2,1)} %param.22) | copy-start | bytes 49156
  27.5 5.7 %copy-start.11 = (f32[4]{0:T(128)S(1)}, f32[4]{0:T(128)}, u32[]{:S(2)}) copy-start(f32[4]{0:T(128)} %param.23) | copy-start | bytes 52
  29.4 112.8 %all-gather.9.cloned.1.call-start = ((), (), s32[]{:S(2)}) async-start(), calls=%async_computation.4 | async-start | bytes 2359296 | tf_op jit(solution)/shard_map/all_gather | solution.py:91
  37.1 7.2 %copy-start.5 = (f32[1,4,2,128]{3,1,2,0:T(4,128)}, f32[1,4,2,128]{3,1,2,0:T(4,128)S(1)}, u32[]{:S(2)}) copy-start(f32[1,4,2,128]{3,1,2,0:T(4,128)S(1)} %copy.67) | copy-start | bytes 12292
  37.8 18.8 %collective-permute-start = (f32[4]{0:T(128)}, f32[4]{0:T(128)}, u32[]{:S(2)}, u32[]{:S(2)}) collective-permute-start(f32[4]{0:T(128)} %exp.49), channel_id=1, source_target_pairs={{14,0},{0,2},{2,4},{4,6},{6,8},{8,10},{10,12},{12,14},{15,1},{1,3}... | collective-permute-start | bytes 56 | tf_op jit(solution)/shard_map/ppermute | solution.py:17
  44.2 9.9 %copy-start.13 = (bf16[32,4,8,128]{3,2,1,0:T(8,128)(2,1)}, bf16[32,4,8,128]{3,2,1,0:T(8,128)(2,1)S(1)}, u32[]{:S(2)}) copy-start(bf16[32,4,8,128]{3,2,1,0:T(8,128)(2,1)S(1)} %fusion.43) | copy-start | bytes 786436
  45.2 28.8 %collective-permute-start.3 = (f32[4,128,64]{1,2,0:T(8,128)}, f32[4,128,64]{1,2,0:T(8,128)S(1)}, u32[]{:S(2)}, u32[]{:S(2)}) collective-permute-start(f32[4,128,64]{1,2,0:T(8,128)} %fusion.35), channel_id=1, source_target_pairs={{14,0},{0,2},{2,4},{4,6},{6,8},{8,10},{10,12},{12,14},{15,1},{1,3}... | collective-permute-start | bytes 393224 | tf_op jit(solution)/shard_map/ppermute | solution.py:17
  48.5 140.6 %reduce-scatter.2.cloned.1.call-start = ((), (), s32[]{:S(2)}) async-start(), calls=%async_computation.3 | async-start | bytes 3145728 | tf_op jit(solution)/shard_map/reduce_scatter | solution.py:202
  49.5 8.8 %collective-permute-start.8 = (f32[4]{0:T(128)}, f32[4]{0:T(128)}, u32[]{:S(2)}, u32[]{:S(2)}) collective-permute-start(f32[4]{0:T(128)} %exp.54), channel_id=1, source_target_pairs={{2,0},{4,2},{6,4},{8,6},{10,8},{12,10},{14,12},{0,14},{3,1},{5,3},... | collective-permute-start | bytes 56 | tf_op jit(solution)/shard_map/ppermute | solution.py:17
  53.8 19.7 %collective-permute-start.11 = (f32[4,128,64]{1,2,0:T(8,128)}, f32[4,128,64]{1,2,0:T(8,128)S(1)}, u32[]{:S(2)}, u32[]{:S(2)}) collective-permute-start(f32[4,128,64]{1,2,0:T(8,128)} %fusion.33), channel_id=1, source_target_pairs={{2,0},{4,2},{6,4},{8,6},{10,8},{12,10},{14,12},{0,14},{3,1},{5,3},... | collective-permute-start | bytes 393224 | tf_op jit(solution)/shard_map/ppermute | solution.py:17
  54.4 1.7 copy-start.14
  54.4 1.7 copy-start.15
  56.6 6.5 %collective-permute-start.1 = (f32[4]{0:T(128)}, f32[4]{0:T(128)S(1)}, u32[]{:S(2)}, u32[]{:S(2)}) collective-permute-start(f32[4]{0:T(128)} %collective-permute-done), channel_id=1, source_target_pairs={{14,0},{0,2},{2,4},{4,6},{6,8},{8,10},{10,12},{12,14},{15,1},{1,3}... | collective-permute-start | bytes 56 | tf_op jit(solution)/shard_map/ppermute | solution.py:17
  58.4 5.4 %collective-permute-start.9 = (f32[4]{0:T(128)}, f32[4]{0:T(128)S(1)}, u32[]{:S(2)}, u32[]{:S(2)}) collective-permute-start(f32[4]{0:T(128)} %collective-permute-done.8), channel_id=1, source_target_pairs={{2,0},{4,2},{6,4},{8,6},{10,8},{12,10},{14,12},{0,14},{3,1},{5,3},... | collective-permute-start | bytes 56 | tf_op jit(solution)/shard_map/ppermute | solution.py:17
  63.8 5.4 %collective-permute-start.2 = (f32[4]{0:T(128)S(1)}, f32[4]{0:T(128)S(1)}, u32[]{:S(2)}, u32[]{:S(2)}) collective-permute-start(f32[4]{0:T(128)S(1)} %mul.277), channel_id=1, source_target_pairs={{12,0},{14,2},{0,4},{2,6},{4,8},{6,10},{8,12},{10,14},{13,1},{15,3... | collective-permute-start | bytes 56 | tf_op jit(solution)/shard_map/ppermute | solution.py:17
  64.4 5.1 %collective-permute-start.10 = (f32[4]{0:T(128)S(1)}, f32[4]{0:T(128)S(1)}, u32[]{:S(2)}, u32[]{:S(2)}) collective-permute-start(f32[4]{0:T(128)S(1)} %mul.298), channel_id=1, source_target_pairs={{4,0},{6,2},{8,4},{10,6},{12,8},{14,10},{0,12},{2,14},{5,1},{7,3},... | collective-permute-start | bytes 56 | tf_op jit(solution)/shard_map/ppermute | solution.py:17
  69.1 4.5 %collective-permute-start.7 = (f32[4]{0:T(128)S(1)}, f32[4]{0:T(128)S(1)}, u32[]{:S(2)}, u32[]{:S(2)}) collective-permute-start(f32[4]{0:T(128)S(1)} %mul.278), channel_id=1, source_target_pairs={{8,0},{10,2},{12,4},{14,6},{0,8},{2,10},{4,12},{6,14},{9,1},{11,3}... | collective-permute-start | bytes 56 | tf_op jit(solution)/shard_map/ppermute | solution.py:17
  69.5 4.4 %collective-permute-start.15 = (f32[4]{0:T(128)S(1)}, f32[4]{0:T(128)S(1)}, u32[]{:S(2)}, u32[]{:S(2)}) collective-permute-start(f32[4]{0:T(128)S(1)} %mul.299), channel_id=1, source_target_pairs={{8,0},{10,2},{12,4},{14,6},{0,8},{2,10},{4,12},{6,14},{9,1},{11,3}... | collective-permute-start | bytes 56 | tf_op jit(solution)/shard_map/ppermute | solution.py:17
  73.6 5.9 %collective-permute-start.12 = (f32[4,128,64]{1,2,0:T(8,128)S(1)}, f32[4,128,64]{1,2,0:T(8,128)S(1)}, u32[]{:S(2)}, u32[]{:S(2)}) collective-permute-start(f32[4,128,64]{1,2,0:T(8,128)S(1)} %collective-permute-done.11), channel_id=1, source_target_pairs={{2,0},{4,2},{6,4},{8,6},{10,8},{12,10},{14,12},{0,14},{3,1},{5,3},... | collective-permute-start | bytes 393224 | tf_op jit(solution)/shard_map/ppermute | solution.py:17
  74.0 11.4 %collective-permute-start.4 = (f32[4,128,64]{1,2,0:T(8,128)S(1)}, f32[4,128,64]{1,2,0:T(8,128)S(1)}, u32[]{:S(2)}, u32[]{:S(2)}) collective-permute-start(f32[4,128,64]{1,2,0:T(8,128)S(1)} %collective-permute-done.3), channel_id=1, source_target_pairs={{14,0},{0,2},{2,4},{4,6},{6,8},{8,10},{10,12},{12,14},{15,1},{1,3}... | collective-permute-start | bytes 393224 | tf_op jit(solution)/shard_map/ppermute | solution.py:17
  80.2 6.4 %collective-permute-start.13 = (f32[4,128,64]{1,2,0:T(8,128)S(1)}, f32[4,128,64]{1,2,0:T(8,128)S(1)}, u32[]{:S(2)}, u32[]{:S(2)}) collective-permute-start(f32[4,128,64]{1,2,0:T(8,128)S(1)} %multiply_add_fusion.1), channel_id=1, source_target_pairs={{4,0},{6,2},{8,4},{10,6},{12,8},{14,10},{0,12},{2,14},{5,1},{7,3},... | collective-permute-start | bytes 393224 | tf_op jit(solution)/shard_map/ppermute | solution.py:17
  86.2 11.8 %collective-permute-start.5 = (f32[4,128,64]{1,2,0:T(8,128)S(1)}, f32[4,128,64]{1,2,0:T(8,128)S(1)}, u32[]{:S(2)}, u32[]{:S(2)}) collective-permute-start(f32[4,128,64]{1,2,0:T(8,128)S(1)} %multiply_add_fusion.3), channel_id=1, source_target_pairs={{12,0},{14,2},{0,4},{2,6},{4,8},{6,10},{8,12},{10,14},{13,1},{15,3... | collective-permute-start | bytes 393224 | tf_op jit(solution)/shard_map/ppermute | solution.py:17
  86.7 14.8 %collective-permute-start.14 = (f32[4,128,64]{1,2,0:T(8,128)S(1)}, f32[4,128,64]{1,2,0:T(8,128)S(1)}, u32[]{:S(2)}, u32[]{:S(2)}) collective-permute-start(f32[4,128,64]{1,2,0:T(8,128)S(1)} %multiply_add_fusion), channel_id=1, source_target_pairs={{8,0},{10,2},{12,4},{14,6},{0,8},{2,10},{4,12},{6,14},{9,1},{11,3}... | collective-permute-start | bytes 393224 | tf_op jit(solution)/shard_map/ppermute | solution.py:17
  98.0 10.2 %collective-permute-start.6 = (f32[4,128,64]{1,2,0:T(8,128)S(1)}, f32[4,128,64]{1,2,0:T(8,128)S(1)}, u32[]{:S(2)}, u32[]{:S(2)}) collective-permute-start(f32[4,128,64]{1,2,0:T(8,128)S(1)} %multiply_add_fusion.2), channel_id=1, source_target_pairs={{8,0},{10,2},{12,4},{14,6},{0,8},{2,10},{4,12},{6,14},{9,1},{11,3}... | collective-permute-start | bytes 393224 | tf_op jit(solution)/shard_map/ppermute | solution.py:17
  146.8 3.4 %copy-start.12 = (s32[4]{0:T(128)S(1)}, s32[4]{0:T(128)}, u32[]{:S(2)}) copy-start(s32[4]{0:T(128)} %iota_multiply_fusion) | copy-start | bytes 52
  150.1 28.6 %copy-start.7 = (f32[512]{0:T(512)S(1)}, f32[512]{0:T(512)}, u32[]{:S(2)}) copy-start(f32[512]{0:T(512)} %param.26) | copy-start | bytes 6148
  150.1 28.6 %copy-start.8 = (f32[512]{0:T(512)S(1)}, f32[512]{0:T(512)}, u32[]{:S(2)}) copy-start(f32[512]{0:T(512)} %param.25) | copy-start | bytes 6148
  181.1 8.0 %copy-start.2 = (bf16[256,1024]{1,0:T(8,128)(2,1)S(1)}, bf16[256,1024]{1,0:T(8,128)(2,1)}, u32[]{:S(2)}) copy-start(bf16[256,1024]{1,0:T(8,128)(2,1)} %param.15) | copy-start | bytes 1572868
Sparse Core Ops, SparseCore 0:
  8.9 11.7 all-gather.4
  29.6 61.0 all-gather.6
  92.7 49.5 all-gather.8
  181.2 7.7 reduce-scatter.1
where the time goes:
time: 199 us; the launch traced here: 198 us
  waiting for transfers between devices  61.6 us (31%)
  matrix products  41.7 us (21%)
  local copies, waits for them, and re-layouts  33.6 us (17%)
  starting transfers between devices  31 us (16%)
  other arithmetic  15.6 us (8%)
  between operations  14.1 us (7%)
    ppermute x16, starting transfers between devices, passed_along(): return lax.ppermute(block, axis, route)  30.9 us
    all_gather x1, waiting for transfers between devices, local(): value_piece = lax.all_gather(valueset, 'seq', axis=0, tiled=True)  24.4 us
    ppermute x16, waiting for transfers between devices, passed_along(): return lax.ppermute(block, axis, route)  24 us
    unnamed x38, local copies, waits for them, and re-layouts  18 us
    dot_general x4, matrix products, key_block(): jnp.einsum('epq,fpq->pef', query_tile_rows, key_fragment, preferred_eleme...  11.6 us
    dot_general x4, matrix products, key_block(): jnp.einsum('gfa,agn->fgn', weights.astype(jnp.bfloat16), value_piece, pre...  9.27 us
    reduce_scatter x1, waiting for transfers between devices, local(): lax.psum_scatter(partial_out, 'chan', scatter_dimension=1, tiled=True)  7.92 us
    lt x4, other arithmetic, key_block(): key_position < valid_limit  5.19 us
  transfers between devices with their start and end apart: 20, of which 13 were waited for; matrix products, arithmetic and copies ran while one was open for 21% of the time, Pallas kernels for 0%

commit v1 on v0

--- a/solution.py
+++ b/solution.py
@@ -88,7 +88,12 @@
     empty_total = jnp.zeros((row_count, head_count), jnp.float32)
     carry_pair = (empty_numer, empty_total)
     key_fragment = lax.all_gather(keyset, "seq", axis=0, tiled=True)
-    value_piece = lax.all_gather(valueset, "seq", axis=0, tiled=True)
+    ring = [valueset]
+    for hop in range(7):
+        ring.append(lax.ppermute(ring[-1], "seq", [(dev, (dev + 1) % 8) for dev in range(8)]))
+    value_piece = jnp.roll(
+        jnp.concatenate(ring[::-1], axis=0), (lax.axis_index("seq") + 1) * ring[0].shape[0], axis=0
+    )
     piece_rows = key_fragment.shape[0]
     block_count = piece_rows // 512
 

time: 199 us -> 210 us (1.055)
  starting transfers between devices: 31 us -> 57.7 us
  waiting for transfers between devices: 61.6 us -> 51.5 us
  matrix products: 41.7 us -> 38.3 us
    all_gather x1 -> x0, waiting for transfers between devices: 24.4 us -> none  [local(): value_piece = lax.all_gather(valueset, 'seq', axis=0, tiled=True)]
    ppermute x0 -> x7, waiting for transfers between devices: none -> 20 us  [local(): lax.ppermute(ring[-1], 'seq', [(dev, (dev + 1) % 8) for dev in range(8)])]
    ppermute x0 -> x7, starting transfers between devices: none -> 17.2 us  [local(): lax.ppermute(ring[-1], 'seq', [(dev, (dev + 1) % 8) for dev in range(8)])]
    ppermute x16, starting transfers between devices: 30.9 us -> 40.4 us  [passed_along(): return lax.ppermute(block, axis, route)]
    dynamic_slice x0 -> x2, local copies, waits for them, and re-layouts: none -> 5.52 us  [local(): jnp.roll(jnp.concatenate(ring[::-1], axis=0), (lax.axis_index('seq') + 1)...]
    reshape x2 -> x1, local copies, waits for them, and re-layouts: 4.52 us -> 0.01 us  [the longest x1 4.5 us: local(): value_piece.reshape(block_count, 512, head_count, HEAD_DIM)]
    ppermute x16, waiting for transfers between devices: 24 us -> 19.6 us  [passed_along(): return lax.ppermute(block, axis, route)]
    unnamed x38 -> x58, local copies, waits for them, and re-layouts: 18 us -> 16.9 us
  transfers between devices with their start and end apart: 20 -> 26, of which waited for: 13 -> 12; matrix products, arithmetic and copies ran while one was open for 21% -> 14% of each run, Pallas kernels for 0% -> 0%
where the time goes in v1:
time: 210 us; the launch traced here: 209 us
  starting transfers between devices  57.7 us (27%)
  waiting for transfers between devices  51.5 us (25%)
  matrix products  38.3 us (18%)
  local copies, waits for them, and re-layouts  32.8 us (16%)
  other arithmetic  14.3 us (7%)
  between operations  14.3 us (7%)
    ppermute x16, starting transfers between devices, passed_along(): return lax.ppermute(block, axis, route)  40.4 us
    ppermute x7, waiting for transfers between devices, local(): lax.ppermute(ring[-1], 'seq', [(dev, (dev + 1) % 8) for dev in range(8)])  20 us
    ppermute x16, waiting for transfers between devices, passed_along(): return lax.ppermute(block, axis, route)  19.6 us
    ppermute x7, starting transfers between devices, local(): lax.ppermute(ring[-1], 'seq', [(dev, (dev + 1) % 8) for dev in range(8)])  17.2 us
    unnamed x58, local copies, waits for them, and re-layouts  16.9 us
    dot_general x4, matrix products, key_block(): jnp.einsum('epq,fpq->pef', query_tile_rows, key_fragment, preferred_eleme...  11.5 us
    dot_general x4, matrix products, key_block(): jnp.einsum('gfa,agn->fgn', weights.astype(jnp.bfloat16), value_piece, pre...  9.48 us
    reduce_scatter x1, waiting for transfers between devices, local(): lax.psum_scatter(partial_out, 'chan', scatter_dimension=1, tiled=True)  8.04 us
  transfers between devices with their start and end apart: 26, of which 12 were waited for; matrix products, arithmetic and copies ran while one was open for 14% of the time, Pallas kernels for 0%

profile of v1, /device:TPU:0, one launch (start us, length us, event | category | flops | bytes accessed | tf_op | source)
XLA Modules:
  0.0 209.1 jit_solution(11069321684514432197)
XLA Ops:
  7.4 8.9 %copy.25 = bf16[2048,3,512]{0,2,1:T(8,128)(2,1)} copy(bf16[2048,3,512]{2,0,1:T(8,128)(2,1)} %param.19) | data formatting | bytes 12582912 | tf_op args[4]
  17.6 3.1 %all-gather.3.cloned.1.call-done = bf16[256,2048]{1,0:T(8,128)(2,1)} async-done(((bf16[256,1024]{1,0:T(8,128)(2,1)}), bf16[256,2048]{1,0:T(8,128)(2,1)}) %all-gather.3.cloned.1.call-update) | async-done | bytes 1048592 | tf_op jit(solution)/shard_map/all_gather | solution.py:71
  20.7 1.7 fusion.13
  22.4 5.1 %fusion.17 = f32[256,3,4,128]{0,3,2,1:T(8,128)S(1)} fusion(bf16[3,4,128,2048]{3,2,1,0:T(8,128)(2,1)} %bitcast.163, bf16[256,2048]{1,0:T(8,128)(2,1)S(1)} %fusion.13), kind=kOutput, calls=%fused_computation.29 | convolution fusion | flops 1610612736 | bytes 8912896 | tf_op jit(solution)/shard_map/dot_general | solution.py:79
  35.5 1.7 collective-permute-start
  37.2 2.0 multiply_convert_fusion.5
  40.1 1.5 collective-permute-start.7
  41.7 1.9 multiply_convert_fusion.7
  43.5 2.7 %fusion.44 = bf16[32,4,8,128]{3,2,1,0:T(8,128)(2,1)S(1)} fusion(bf16[256,2048]{1,0:T(8,128)(2,1)} %copy-done.2, bf16[2048,512]{1,0:T(8,128)(2,1)} %param.20), kind=kOutput, calls=%fused_computation.73 | convolution fusion | flops 537526272 | bytes 3407872 | tf_op jit(solution)/shard_map/dot_general | solution.py:125
  46.7 1.5 collective-permute-start.10
  48.2 3.2 %collective-permute-start.15 = (f32[4]{0:T(128)S(1)}, f32[4]{0:T(128)S(1)}, u32[]{:S(2)}, u32[]{:S(2)}) collective-permute-start(f32[4]{0:T(128)S(1)} %exp.54), channel_id=1, source_target_pairs={{2,0},{4,2},{6,4},{8,6},{10,8},{12,10},{14,12},{0,14},{3,1},{5,3},... | collective-permute-start | bytes 56 | tf_op jit(solution)/shard_map/ppermute | solution.py:17
  52.1 4.8 %collective-permute-start.18 = (f32[4,128,64]{1,2,0:T(8,128)S(1)}, f32[4,128,64]{1,2,0:T(8,128)S(1)}, u32[]{:S(2)}, u32[]{:S(2)}) collective-permute-start(f32[4,128,64]{1,2,0:T(8,128)S(1)} %fusion.34), channel_id=1, source_target_pairs={{2,0},{4,2},{6,4},{8,6},{10,8},{12,10},{14,12},{0,14},{3,1},{5,3},... | collective-permute-start | bytes 393224 | tf_op jit(solution)/shard_map/ppermute | solution.py:17
  57.4 8.6 %collective-permute-done.1 = bf16[256,4,128]{0,2,1:T(8,128)(2,1)S(1)} collective-permute-done((bf16[256,4,128]{0,2,1:T(8,128)(2,1)S(1)}, bf16[256,4,128]{0,2,1:T(8,128)(2,1)S(1)}, u32[]{:S(2)}, u32[]{:S(2)}) %collective-permute-start.1) | collective-permute-done | bytes 262176 | tf_op jit(solution)/shard_map/ppermute | solution.py:93
  67.6 3.8 %collective-permute-start.16 = (f32[4]{0:T(128)S(1)}, f32[4]{0:T(128)S(1)}, u32[]{:S(2)}, u32[]{:S(2)}) collective-permute-start(f32[4]{0:T(128)S(1)} %collective-permute-done.15), channel_id=1, source_target_pairs={{2,0},{4,2},{6,4},{8,6},{10,8},{12,10},{14,12},{0,14},{3,1},{5,3},... | collective-permute-start | bytes 56 | tf_op jit(solution)/shard_map/ppermute | solution.py:17
  71.4 4.6 %collective-permute-done.8 = f32[4]{0:T(128)S(1)} collective-permute-done((f32[4]{0:T(128)S(1)}, f32[4]{0:T(128)S(1)}, u32[]{:S(2)}, u32[]{:S(2)}) %collective-permute-start.8) | collective-permute-done | bytes 48 | tf_op jit(solution)/shard_map/ppermute | solution.py:17
  76.0 3.8 %collective-permute-start.17 = (f32[4]{0:T(128)S(1)}, f32[4]{0:T(128)S(1)}, u32[]{:S(2)}, u32[]{:S(2)}) collective-permute-start(f32[4]{0:T(128)S(1)} %mul.302), channel_id=1, source_target_pairs={{4,0},{6,2},{8,4},{10,6},{12,8},{14,10},{0,12},{2,14},{5,1},{7,3},... | collective-permute-start | bytes 56 | tf_op jit(solution)/shard_map/ppermute | solution.py:17
  79.8 1.6 collective-permute-done.9
  81.4 2.9 %collective-permute-start.22 = (f32[4]{0:T(128)S(1)}, f32[4]{0:T(128)S(1)}, u32[]{:S(2)}, u32[]{:S(2)}) collective-permute-start(f32[4]{0:T(128)S(1)} %mul.303), channel_id=1, source_target_pairs={{8,0},{10,2},{12,4},{14,6},{0,8},{2,10},{4,12},{6,14},{9,1},{11,3}... | collective-permute-start | bytes 56 | tf_op jit(solution)/shard_map/ppermute | solution.py:17
  84.3 1.5 collective-permute-done.14
  85.8 2.0 collective-permute-start.3
  87.9 6.4 %collective-permute-done.19 = f32[4,128,64]{1,2,0:T(8,128)S(1)} collective-permute-done((f32[4,128,64]{1,2,0:T(8,128)S(1)}, f32[4,128,64]{1,2,0:T(8,128)S(1)}, u32[]{:S(2)}, u32[]{:S(2)}) %collective-permute-start.19) | collective-permute-done | bytes 131104 | tf_op jit(solution)/shard_map/ppermute | solution.py:17
  94.4 7.1 %collective-permute-start.20 = (f32[4,128,64]{1,2,0:T(8,128)S(1)}, f32[4,128,64]{1,2,0:T(8,128)S(1)}, u32[]{:S(2)}, u32[]{:S(2)}) collective-permute-start(f32[4,128,64]{1,2,0:T(8,128)S(1)} %multiply_add_fusion.1), channel_id=1, source_target_pairs={{4,0},{6,2},{8,4},{10,6},{12,8},{14,10},{0,12},{2,14},{5,1},{7,3},... | collective-permute-start | bytes 393224 | tf_op jit(solution)/shard_map/ppermute | solution.py:17
  103.4 4.8 %collective-permute-done.20 = f32[4,128,64]{1,2,0:T(8,128)S(1)} collective-permute-done((f32[4,128,64]{1,2,0:T(8,128)S(1)}, f32[4,128,64]{1,2,0:T(8,128)S(1)}, u32[]{:S(2)}, u32[]{:S(2)}) %collective-permute-start.20) | collective-permute-done | bytes 131104 | tf_op jit(solution)/shard_map/ppermute | solution.py:17
  108.3 6.6 %collective-permute-start.21 = (f32[4,128,64]{1,2,0:T(8,128)S(1)}, f32[4,128,64]{1,2,0:T(8,128)S(1)}, u32[]{:S(2)}, u32[]{:S(2)}) collective-permute-start(f32[4,128,64]{1,2,0:T(8,128)S(1)} %multiply_add_fusion), channel_id=1, source_target_pairs={{8,0},{10,2},{12,4},{14,6},{0,8},{2,10},{4,12},{6,14},{9,1},{11,3}... | collective-permute-start | bytes 393224 | tf_op jit(solution)/shard_map/ppermute | solution.py:17
  115.6 2.3 %collective-permute-start.5 = (bf16[256,4,128]{0,2,1:T(8,128)(2,1)S(1)}, bf16[256,4,128]{0,2,1:T(8,128)(2,1)S(1)}, u32[]{:S(2)}, u32[]{:S(2)}) collective-permute-start(bf16[256,4,128]{0,2,1:T(8,128)(2,1)S(1)} %collective-permute-done.4), channel_id=1, source_target_pairs={{0,2},{2,4},{4,6},{6,8},{8,10},{10,12},{12,14},{14,0},{1,3},{3,5},... | collective-permute-start | bytes 786440 | tf_op jit(solution)/shard_map/ppermute | solution.py:93
  118.0 2.9 %collective-permute-start.13 = (f32[4,128,64]{1,2,0:T(8,128)S(1)}, f32[4,128,64]{1,2,0:T(8,128)S(1)}, u32[]{:S(2)}, u32[]{:S(2)}) collective-permute-start(f32[4,128,64]{1,2,0:T(8,128)S(1)} %multiply_add_fusion.2), channel_id=1, source_target_pairs={{8,0},{10,2},{12,4},{14,6},{0,8},{2,10},{4,12},{6,14},{9,1},{11,3}... | collective-permute-start | bytes 393224 | tf_op jit(solution)/shard_map/ppermute | solution.py:17
  121.4 5.4 %collective-permute-done.5 = bf16[256,4,128]{0,2,1:T(8,128)(2,1)S(1)} collective-permute-done((bf16[256,4,128]{0,2,1:T(8,128)(2,1)S(1)}, bf16[256,4,128]{0,2,1:T(8,128)(2,1)S(1)}, u32[]{:S(2)}, u32[]{:S(2)}) %collective-permute-start.5) | collective-permute-done | bytes 262176 | tf_op jit(solution)/shard_map/ppermute | solution.py:93
  126.8 11.2 %collective-permute-start.6 = (bf16[256,4,128]{0,2,1:T(8,128)(2,1)S(1)}, bf16[256,4,128]{0,2,1:T(8,128)(2,1)S(1)}, u32[]{:S(2)}, u32[]{:S(2)}) collective-permute-start(bf16[256,4,128]{0,2,1:T(8,128)(2,1)S(1)} %collective-permute-done.5), channel_id=1, source_target_pairs={{0,2},{2,4},{4,6},{6,8},{8,10},{10,12},{12,14},{14,0},{1,3},{3,5},... | collective-permute-start | bytes 786440 | tf_op jit(solution)/shard_map/ppermute | solution.py:93
  138.5 5.3 %collective-permute-done.6 = bf16[256,4,128]{0,2,1:T(8,128)(2,1)S(1)} collective-permute-done((bf16[256,4,128]{0,2,1:T(8,128)(2,1)S(1)}, bf16[256,4,128]{0,2,1:T(8,128)(2,1)S(1)}, u32[]{:S(2)}, u32[]{:S(2)}) %collective-permute-start.6) | collective-permute-done | bytes 262176 | tf_op jit(solution)/shard_map/ppermute | solution.py:93
  146.5 1.6 constant_dynamic-slice_fusion
  148.1 3.9 %copy.26 = bf16[2048,4,128]{2,0,1:T(8,128)(2,1)} copy(bf16[2048,4,128]{0,2,1:T(8,128)(2,1)} %constant_dynamic-slice_fusion) | data formatting | bytes 4194304 | tf_op jit(solution)/shard_map/jit(_roll_dynamic)/dynamic_slice | solution.py:94
  152.0 4.6 %reshape.152 = bf16[4,512,4,128]{1,0,3,2:T(4,128)(2,1)} reshape(bf16[2048,4,128]{0,2,1:T(8,128)(2,1)} %all-gather.5.cloned.1.call-done) | data formatting | bytes 4194304 | tf_op jit(solution)/shard_map/reshape | solution.py:117
  156.5 4.5 %copy.28 = bf16[4,512,4,128]{3,1,2,0:T(8,128)(2,1)} copy(bf16[4,512,4,128]{1,0,3,2:T(4,128)(2,1)} %reshape.152) | data formatting | bytes 4194304
  161.1 28.7 %while.13 = (s32[]{:T(128)}, f32[256,4,128]{0,2,1:T(8,128)S(1)}, f32[256,4]{0,1:T(4,128)S(1)}, bf16[4,512,4,128]{3,1,0,2:T(8,128)(2,1)}, s32[4]{0:T(128)S(1)}, /...) while((s32[]{:T(128)}, f32[256,4,128]{0,2,1:T(8,128)S(1)}, ...), condition=%wide.region_4.5_spmd.clone, body=%wide.region_2.4_spmd.clone.sunk | while | flops 271845376 | bytes 6572676 | solution.py:113
  161.7 1.3 add_compare_fusion.2
  163.0 2.9 %bitcast_reduce_fusion.2 = (f32[4,256]{1,0:T(4,128)S(1)}, f32[4,512,256]{2,1,0:T(8,128)}) fusion(pred[512]{0:T(512)(128)(4,1)S(1)} %add_compare_fusion.2, bf16[256,4,128]{2,0,1:T(8,128)(2,1)S(1)} %get-tuple-element.209, bf16[4,512,4,128]{3,1,2,0:T(8,128)(2,1)} %get-tuple-element.208, s32[]{:T(128)} %get-tuple-element.192), kind=kOutput, calls=%fused_computation.clone.1 | convolution fusion | flops 135789568 | bytes 2888704 | tf_op jit(solution)/shard_map/while/body/eval_jaxpr/epq,fpq->pef/dot_general | solution.py:33
  165.9 2.4 %fusion.95 = f32[256,4,128]{0,2,1:T(8,128)S(1)} fusion(f32[4,512,256]{2,1,0:T(8,128)} %get-tuple-element.180, pred[512]{0:T(512)(128)(4,1)S(1)} %add_compare_fusion.2, f32[256,4,128]{0,2,1:T(8,128)S(1)} %get-tuple-element.193, bf16[4,512,4,128]{3,1,0,2:T(8,128)(2,1)} %get-tuple-element.205, s32[]{:T(128)} %get-tuple-element.192, pred[]{:T(512)S(6)} %compare.4), kind=kOutput, calls=%fused_computation.4.clone.1 | convolution fusion | flops 136052736 | bytes 3671041 | tf_op jit(solution)/shard_map/while/body/eval_jaxpr/gfa,agn->fgn/dot_general | solution.py:40
  168.9 1.3 add_compare_fusion.2
  170.2 2.9 %bitcast_reduce_fusion.2 = (f32[4,256]{1,0:T(4,128)S(1)}, f32[4,512,256]{2,1,0:T(8,128)}) fusion(pred[512]{0:T(512)(128)(4,1)S(1)} %add_compare_fusion.2, bf16[256,4,128]{2,0,1:T(8,128)(2,1)S(1)} %get-tuple-element.209, bf16[4,512,4,128]{3,1,2,0:T(8,128)(2,1)} %get-tuple-element.208, s32[]{:T(128)} %get-tuple-element.192), kind=kOutput, calls=%fused_computation.clone.1 | convolution fusion | flops 135789568 | bytes 2888704 | tf_op jit(solution)/shard_map/while/body/eval_jaxpr/epq,fpq->pef/dot_general | solution.py:33
  173.0 2.4 %fusion.95 = f32[256,4,128]{0,2,1:T(8,128)S(1)} fusion(f32[4,512,256]{2,1,0:T(8,128)} %get-tuple-element.180, pred[512]{0:T(512)(128)(4,1)S(1)} %add_compare_fusion.2, f32[256,4,128]{0,2,1:T(8,128)S(1)} %get-tuple-element.193, bf16[4,512,4,128]{3,1,0,2:T(8,128)(2,1)} %get-tuple-element.205, s32[]{:T(128)} %get-tuple-element.192, pred[]{:T(512)S(6)} %compare.4), kind=kOutput, calls=%fused_computation.4.clone.1 | convolution fusion | flops 136052736 | bytes 3671041 | tf_op jit(solution)/shard_map/while/body/eval_jaxpr/gfa,agn->fgn/dot_general | solution.py:40
  176.0 1.3 add_compare_fusion.2
  177.3 2.9 %bitcast_reduce_fusion.2 = (f32[4,256]{1,0:T(4,128)S(1)}, f32[4,512,256]{2,1,0:T(8,128)}) fusion(pred[512]{0:T(512)(128)(4,1)S(1)} %add_compare_fusion.2, bf16[256,4,128]{2,0,1:T(8,128)(2,1)S(1)} %get-tuple-element.209, bf16[4,512,4,128]{3,1,2,0:T(8,128)(2,1)} %get-tuple-element.208, s32[]{:T(128)} %get-tuple-element.192), kind=kOutput, calls=%fused_computation.clone.1 | convolution fusion | flops 135789568 | bytes 2888704 | tf_op jit(solution)/shard_map/while/body/eval_jaxpr/epq,fpq->pef/dot_general | solution.py:33
  180.2 2.4 %fusion.95 = f32[256,4,128]{0,2,1:T(8,128)S(1)} fusion(f32[4,512,256]{2,1,0:T(8,128)} %get-tuple-element.180, pred[512]{0:T(512)(128)(4,1)S(1)} %add_compare_fusion.2, f32[256,4,128]{0,2,1:T(8,128)S(1)} %get-tuple-element.193, bf16[4,512,4,128]{3,1,0,2:T(8,128)(2,1)} %get-tuple-element.205, s32[]{:T(128)} %get-tuple-element.192, pred[]{:T(512)S(6)} %compare.4), kind=kOutput, calls=%fused_computation.4.clone.1 | convolution fusion | flops 136052736 | bytes 3671041 | tf_op jit(solution)/shard_map/while/body/eval_jaxpr/gfa,agn->fgn/dot_general | solution.py:40
  184.5 2.9 %bitcast_reduce_fusion.2 = (f32[4,256]{1,0:T(4,128)S(1)}, f32[4,512,256]{2,1,0:T(8,128)}) fusion(pred[512]{0:T(512)(128)(4,1)S(1)} %add_compare_fusion.2, bf16[256,4,128]{2,0,1:T(8,128)(2,1)S(1)} %get-tuple-element.209, bf16[4,512,4,128]{3,1,2,0:T(8,128)(2,1)} %get-tuple-element.208, s32[]{:T(128)} %get-tuple-element.192), kind=kOutput, calls=%fused_computation.clone.1 | convolution fusion | flops 135789568 | bytes 2888704 | tf_op jit(solution)/shard_map/while/body/eval_jaxpr/epq,fpq->pef/dot_general | solution.py:33
  187.4 2.4 %fusion.95 = f32[256,4,128]{0,2,1:T(8,128)S(1)} fusion(f32[4,512,256]{2,1,0:T(8,128)} %get-tuple-element.180, pred[512]{0:T(512)(128)(4,1)S(1)} %add_compare_fusion.2, f32[256,4,128]{0,2,1:T(8,128)S(1)} %get-tuple-element.193, bf16[4,512,4,128]{3,1,0,2:T(8,128)(2,1)} %get-tuple-element.205, s32[]{:T(128)} %get-tuple-element.192, pred[]{:T(512)S(6)} %compare.4), kind=kOutput, calls=%fused_computation.4.clone.1 | convolution fusion | flops 136052736 | bytes 3671041 | tf_op jit(solution)/shard_map/while/body/eval_jaxpr/gfa,agn->fgn/dot_general | solution.py:40
  190.1 2.1 fusion.78
  192.2 8.0 %reduce-scatter.2.cloned.1.call-done = f32[256,1024]{1,0:T(8,128)} async-done(((f32[256,2048]{1,0:T(8,128)}), f32[256,1024]{1,0:T(8,128)}) %reduce-scatter.2.cloned.1.call-update) | async-done | bytes 1048592 | tf_op jit(solution)/shard_map/reduce_scatter | solution.py:207
  200.2 2.3 %add_convert_fusion = bf16[256,1024]{1,0:T(8,128)(2,1)} fusion(f32[256,1024]{1,0:T(8,128)} %reduce-scatter.2.cloned.1.call-done, bf16[256,1024]{1,0:T(8,128)(2,1)} %param.15), kind=kLoop, calls=%fused_computation.31 | loop fusion | flops 786432 | bytes 2097152 | tf_op jit(solution)/shard_map/convert_element_type | solution.py:208
  (154 shorter events, 24.0 us)
Async XLA Ops:
  6.5 183.6 %copy-start = (bf16[512,2048]{1,0:T(8,128)(2,1)S(1)}, bf16[512,2048]{1,0:T(8,128)(2,1)}, u32[]{:S(2)}) copy-start(bf16[512,2048]{1,0:T(8,128)(2,1)} %param.27) | copy-start | bytes 6291460
  6.5 14.1 %all-gather.3.cloned.1.call-start = ((), (), s32[]{:S(2)}) async-start(), calls=%async_computation.1 | async-start | bytes 1572864 | tf_op jit(solution)/shard_map/all_gather | solution.py:71
  7.3 144.7 %all-gather.5.cloned.1.call-start = ((), (), s32[]{:S(2)}) async-start(), calls=%async_computation.2 | async-start | bytes 2359296 | tf_op jit(solution)/shard_map/all_gather | solution.py:90
  7.3 9.6 %copy-start.15 = (f32[4]{0:T(128)S(1)}, f32[4]{0:T(128)}, u32[]{:S(2)}) copy-start(f32[4]{0:T(128)} %param.24) | copy-start | bytes 52
  7.4 10.2 %copy-start.9 = (s32[256]{0:T(256)S(1)}, s32[256]{0:T(256)}, u32[]{:S(2)}) copy-start(s32[256]{0:T(256)} %param.16) | copy-start | bytes 3076
  7.4 13.3 %copy-start.4 = (bf16[16,2048]{1,0:T(8,128)(2,1)S(1)}, bf16[16,2048]{1,0:T(8,128)(2,1)}, u32[]{:S(2)}) copy-start(bf16[16,2048]{1,0:T(8,128)(2,1)} %param.18) | copy-start | bytes 196612
  17.5 14.6 %copy-start.5 = (f32[256]{0:T(256)}, f32[256]{0:T(256)S(1)}, u32[]{:S(2)}) copy-start(f32[256]{0:T(256)S(1)} %compare_convert_fusion) | copy-start | bytes 3076
  22.4 6.4 %copy-start.2 = (bf16[256,2048]{1,0:T(8,128)(2,1)}, bf16[256,2048]{1,0:T(8,128)(2,1)S(1)}, u32[]{:S(2)}) copy-start(bf16[256,2048]{1,0:T(8,128)(2,1)S(1)} %fusion.13) | copy-start | bytes 3145732
  22.4 6.4 %copy-start.14 = (bf16[2048,4]{0,1:T(4,128)(2,1)S(1)}, bf16[2048,4]{0,1:T(4,128)(2,1)}, u32[]{:S(2)}) copy-start(bf16[2048,4]{0,1:T(4,128)(2,1)} %param.22) | copy-start | bytes 49156
  22.4 6.3 %copy-start.16 = (f32[4]{0:T(128)S(1)}, f32[4]{0:T(128)}, u32[]{:S(2)}) copy-start(f32[4]{0:T(128)} %param.23) | copy-start | bytes 52
  27.5 1.2 copy-start.1
  31.4 0.8 copy-start.7
  35.5 16.2 %collective-permute-start = (bf16[256,4,128]{0,2,1:T(8,128)(2,1)S(1)}, bf16[256,4,128]{0,2,1:T(8,128)(2,1)S(1)}, u32[]{:S(2)}, u32[]{:S(2)}) collective-permute-start(bf16[256,4,128]{0,2,1:T(8,128)(2,1)S(1)} %fusion.33), channel_id=1, source_target_pairs={{0,2},{2,4},{4,6},{6,8},{8,10},{10,12},{12,14},{14,0},{1,3},{3,5},... | collective-permute-start | bytes 786440 | tf_op jit(solution)/shard_map/ppermute | solution.py:93
  39.2 161.0 %reduce-scatter.2.cloned.1.call-start = ((), (), s32[]{:S(2)}) async-start(), calls=%async_computation.3 | async-start | bytes 3145728 | tf_op jit(solution)/shard_map/reduce_scatter | solution.py:207
  40.1 6.1 %copy-start.13 = (f32[4]{0:T(128)S(1)}, f32[4]{0:T(128)}, u32[]{:S(2)}) copy-start(f32[4]{0:T(128)} %slice_reduce_fusion) | copy-start | bytes 52
  40.1 6.1 %copy-start.6 = (f32[256]{0:T(256)S(1)}, f32[256]{0:T(256)}, u32[]{:S(2)}) copy-start(f32[256]{0:T(256)} %copy-done.5) | copy-start | bytes 3076
  40.1 6.2 %copy-start.10 = (f32[256,4]{0,1:T(4,128)S(1)}, f32[256,4]{0,1:T(4,128)}, u32[]{:S(2)}) copy-start(f32[256,4]{0,1:T(4,128)} %get-tuple-element.115) | copy-start | bytes 12292
  40.1 16.7 %copy-start.8 = (f32[1,4,2,128]{3,1,2,0:T(4,128)S(1)}, f32[1,4,2,128]{3,1,2,0:T(4,128)}, u32[]{:S(2)}) copy-start(f32[1,4,2,128]{3,1,2,0:T(4,128)} %copy-done.7) | copy-start | bytes 12292
  40.1 16.7 %copy-start.18 = (f32[4,256]{1,0:T(4,128)S(1)}, f32[4,256]{1,0:T(4,128)}, u32[]{:S(2)}) copy-start(f32[4,256]{1,0:T(4,128)} %get-tuple-element.118) | copy-start | bytes 12292
  40.1 26.4 %collective-permute-start.7 = (f32[4]{0:T(128)}, f32[4]{0:T(128)S(1)}, u32[]{:S(2)}, u32[]{:S(2)}) collective-permute-start(f32[4]{0:T(128)} %exp.49), channel_id=1, source_target_pairs={{14,0},{0,2},{2,4},{4,6},{6,8},{8,10},{10,12},{12,14},{15,1},{1,3}... | collective-permute-start | bytes 56 | tf_op jit(solution)/shard_map/ppermute | solution.py:17
  46.7 41.2 %collective-permute-start.10 = (f32[4,128,64]{1,2,0:T(8,128)S(1)}, f32[4,128,64]{1,2,0:T(8,128)S(1)}, u32[]{:S(2)}, u32[]{:S(2)}) collective-permute-start(f32[4,128,64]{1,2,0:T(8,128)S(1)} %fusion.36), channel_id=1, source_target_pairs={{14,0},{0,2},{2,4},{4,6},{6,8},{8,10},{10,12},{12,14},{15,1},{1,3}... | collective-permute-start | bytes 393224 | tf_op jit(solution)/shard_map/ppermute | solution.py:17
  48.2 19.4 %collective-permute-start.15 = (f32[4]{0:T(128)S(1)}, f32[4]{0:T(128)S(1)}, u32[]{:S(2)}, u32[]{:S(2)}) collective-permute-start(f32[4]{0:T(128)S(1)} %exp.54), channel_id=1, source_target_pairs={{2,0},{4,2},{6,4},{8,6},{10,8},{12,10},{14,12},{0,14},{3,1},{5,3},... | collective-permute-start | bytes 56 | tf_op jit(solution)/shard_map/ppermute | solution.py:17
  51.7 14.3 %collective-permute-start.1 = (bf16[256,4,128]{0,2,1:T(8,128)(2,1)S(1)}, bf16[256,4,128]{0,2,1:T(8,128)(2,1)S(1)}, u32[]{:S(2)}, u32[]{:S(2)}) collective-permute-start(bf16[256,4,128]{0,2,1:T(8,128)(2,1)S(1)} %collective-permute-done), channel_id=1, source_target_pairs={{0,2},{2,4},{4,6},{6,8},{8,10},{10,12},{12,14},{14,0},{1,3},{3,5},... | collective-permute-start | bytes 786440 | tf_op jit(solution)/shard_map/ppermute | solution.py:93
  52.1 33.7 %collective-permute-start.18 = (f32[4,128,64]{1,2,0:T(8,128)S(1)}, f32[4,128,64]{1,2,0:T(8,128)S(1)}, u32[]{:S(2)}, u32[]{:S(2)}) collective-permute-start(f32[4,128,64]{1,2,0:T(8,128)S(1)} %fusion.34), channel_id=1, source_target_pairs={{2,0},{4,2},{6,4},{8,6},{10,8},{12,10},{14,12},{0,14},{3,1},{5,3},... | collective-permute-start | bytes 393224 | tf_op jit(solution)/shard_map/ppermute | solution.py:17
  66.0 19.9 %collective-permute-start.2 = (bf16[256,4,128]{0,2,1:T(8,128)(2,1)S(1)}, bf16[256,4,128]{0,2,1:T(8,128)(2,1)S(1)}, u32[]{:S(2)}, u32[]{:S(2)}) collective-permute-start(bf16[256,4,128]{0,2,1:T(8,128)(2,1)S(1)} %collective-permute-done.1), channel_id=1, source_target_pairs={{0,2},{2,4},{4,6},{6,8},{8,10},{10,12},{12,14},{14,0},{1,3},{3,5},... | collective-permute-start | bytes 786440 | tf_op jit(solution)/shard_map/ppermute | solution.py:93
  66.5 9.5 %collective-permute-start.8 = (f32[4]{0:T(128)S(1)}, f32[4]{0:T(128)S(1)}, u32[]{:S(2)}, u32[]{:S(2)}) collective-permute-start(f32[4]{0:T(128)S(1)} %collective-permute-done.7), channel_id=1, source_target_pairs={{14,0},{0,2},{2,4},{4,6},{6,8},{8,10},{10,12},{12,14},{15,1},{1,3}... | collective-permute-start | bytes 56 | tf_op jit(solution)/shard_map/ppermute | solution.py:17
  67.6 8.4 %collective-permute-start.16 = (f32[4]{0:T(128)S(1)}, f32[4]{0:T(128)S(1)}, u32[]{:S(2)}, u32[]{:S(2)}) collective-permute-start(f32[4]{0:T(128)S(1)} %collective-permute-done.15), channel_id=1, source_target_pairs={{2,0},{4,2},{6,4},{8,6},{10,8},{12,10},{14,12},{0,14},{3,1},{5,3},... | collective-permute-start | bytes 56 | tf_op jit(solution)/shard_map/ppermute | solution.py:17
  76.0 5.4 %collective-permute-start.9 = (f32[4]{0:T(128)S(1)}, f32[4]{0:T(128)S(1)}, u32[]{:S(2)}, u32[]{:S(2)}) collective-permute-start(f32[4]{0:T(128)S(1)} %mul.281), channel_id=1, source_target_pairs={{12,0},{14,2},{0,4},{2,6},{4,8},{6,10},{8,12},{10,14},{13,1},{15,3... | collective-permute-start | bytes 56 | tf_op jit(solution)/shard_map/ppermute | solution.py:17
  76.0 5.4 %collective-permute-start.17 = (f32[4]{0:T(128)S(1)}, f32[4]{0:T(128)S(1)}, u32[]{:S(2)}, u32[]{:S(2)}) collective-permute-start(f32[4]{0:T(128)S(1)} %mul.302), channel_id=1, source_target_pairs={{4,0},{6,2},{8,4},{10,6},{12,8},{14,10},{0,12},{2,14},{5,1},{7,3},... | collective-permute-start | bytes 56 | tf_op jit(solution)/shard_map/ppermute | solution.py:17
  81.4 4.4 %collective-permute-start.14 = (f32[4]{0:T(128)S(1)}, f32[4]{0:T(128)S(1)}, u32[]{:S(2)}, u32[]{:S(2)}) collective-permute-start(f32[4]{0:T(128)S(1)} %mul.282), channel_id=1, source_target_pairs={{8,0},{10,2},{12,4},{14,6},{0,8},{2,10},{4,12},{6,14},{9,1},{11,3}... | collective-permute-start | bytes 56 | tf_op jit(solution)/shard_map/ppermute | solution.py:17
  81.4 6.5 %collective-permute-start.22 = (f32[4]{0:T(128)S(1)}, f32[4]{0:T(128)S(1)}, u32[]{:S(2)}, u32[]{:S(2)}) collective-permute-start(f32[4]{0:T(128)S(1)} %mul.303), channel_id=1, source_target_pairs={{8,0},{10,2},{12,4},{14,6},{0,8},{2,10},{4,12},{6,14},{9,1},{11,3}... | collective-permute-start | bytes 56 | tf_op jit(solution)/shard_map/ppermute | solution.py:17
  85.8 8.5 %collective-permute-start.19 = (f32[4,128,64]{1,2,0:T(8,128)S(1)}, f32[4,128,64]{1,2,0:T(8,128)S(1)}, u32[]{:S(2)}, u32[]{:S(2)}) collective-permute-start(f32[4,128,64]{1,2,0:T(8,128)S(1)} %collective-permute-done.18), channel_id=1, source_target_pairs={{2,0},{4,2},{6,4},{8,6},{10,8},{12,10},{14,12},{0,14},{3,1},{5,3},... | collective-permute-start | bytes 393224 | tf_op jit(solution)/shard_map/ppermute | solution.py:17
  85.8 15.7 %collective-permute-start.3 = (bf16[256,4,128]{0,2,1:T(8,128)(2,1)S(1)}, bf16[256,4,128]{0,2,1:T(8,128)(2,1)S(1)}, u32[]{:S(2)}, u32[]{:S(2)}) collective-permute-start(bf16[256,4,128]{0,2,1:T(8,128)(2,1)S(1)} %collective-permute-done.2), channel_id=1, source_target_pairs={{0,2},{2,4},{4,6},{6,8},{8,10},{10,12},{12,14},{14,0},{1,3},{3,5},... | collective-permute-start | bytes 786440 | tf_op jit(solution)/shard_map/ppermute | solution.py:93
  87.9 14.4 %collective-permute-start.11 = (f32[4,128,64]{1,2,0:T(8,128)S(1)}, f32[4,128,64]{1,2,0:T(8,128)S(1)}, u32[]{:S(2)}, u32[]{:S(2)}) collective-permute-start(f32[4,128,64]{1,2,0:T(8,128)S(1)} %collective-permute-done.10), channel_id=1, source_target_pairs={{14,0},{0,2},{2,4},{4,6},{6,8},{8,10},{10,12},{12,14},{15,1},{1,3}... | collective-permute-start | bytes 393224 | tf_op jit(solution)/shard_map/ppermute | solution.py:17
  94.4 13.7 %collective-permute-start.20 = (f32[4,128,64]{1,2,0:T(8,128)S(1)}, f32[4,128,64]{1,2,0:T(8,128)S(1)}, u32[]{:S(2)}, u32[]{:S(2)}) collective-permute-start(f32[4,128,64]{1,2,0:T(8,128)S(1)} %multiply_add_fusion.1), channel_id=1, source_target_pairs={{4,0},{6,2},{8,4},{10,6},{12,8},{14,10},{0,12},{2,14},{5,1},{7,3},... | collective-permute-start | bytes 393224 | tf_op jit(solution)/shard_map/ppermute | solution.py:17
  101.6 14.1 %collective-permute-start.4 = (bf16[256,4,128]{0,2,1:T(8,128)(2,1)S(1)}, bf16[256,4,128]{0,2,1:T(8,128)(2,1)S(1)}, u32[]{:S(2)}, u32[]{:S(2)}) collective-permute-start(bf16[256,4,128]{0,2,1:T(8,128)(2,1)S(1)} %collective-permute-done.3), channel_id=1, source_target_pairs={{0,2},{2,4},{4,6},{6,8},{8,10},{10,12},{12,14},{14,0},{1,3},{3,5},... | collective-permute-start | bytes 786440 | tf_op jit(solution)/shard_map/ppermute | solution.py:93
  102.3 15.6 %collective-permute-start.12 = (f32[4,128,64]{1,2,0:T(8,128)S(1)}, f32[4,128,64]{1,2,0:T(8,128)S(1)}, u32[]{:S(2)}, u32[]{:S(2)}) collective-permute-start(f32[4,128,64]{1,2,0:T(8,128)S(1)} %multiply_add_fusion.3), channel_id=1, source_target_pairs={{12,0},{14,2},{0,4},{2,6},{4,8},{6,10},{8,12},{10,14},{13,1},{15,3... | collective-permute-start | bytes 393224 | tf_op jit(solution)/shard_map/ppermute | solution.py:17
  108.3 12.6 %collective-permute-start.21 = (f32[4,128,64]{1,2,0:T(8,128)S(1)}, f32[4,128,64]{1,2,0:T(8,128)S(1)}, u32[]{:S(2)}, u32[]{:S(2)}) collective-permute-start(f32[4,128,64]{1,2,0:T(8,128)S(1)} %multiply_add_fusion), channel_id=1, source_target_pairs={{8,0},{10,2},{12,4},{14,6},{0,8},{2,10},{4,12},{6,14},{9,1},{11,3}... | collective-permute-start | bytes 393224 | tf_op jit(solution)/shard_map/ppermute | solution.py:17
  115.6 11.2 %collective-permute-start.5 = (bf16[256,4,128]{0,2,1:T(8,128)(2,1)S(1)}, bf16[256,4,128]{0,2,1:T(8,128)(2,1)S(1)}, u32[]{:S(2)}, u32[]{:S(2)}) collective-permute-start(bf16[256,4,128]{0,2,1:T(8,128)(2,1)S(1)} %collective-permute-done.4), channel_id=1, source_target_pairs={{0,2},{2,4},{4,6},{6,8},{8,10},{10,12},{12,14},{14,0},{1,3},{3,5},... | collective-permute-start | bytes 786440 | tf_op jit(solution)/shard_map/ppermute | solution.py:93
  118.0 20.0 %collective-permute-start.13 = (f32[4,128,64]{1,2,0:T(8,128)S(1)}, f32[4,128,64]{1,2,0:T(8,128)S(1)}, u32[]{:S(2)}, u32[]{:S(2)}) collective-permute-start(f32[4,128,64]{1,2,0:T(8,128)S(1)} %multiply_add_fusion.2), channel_id=1, source_target_pairs={{8,0},{10,2},{12,4},{14,6},{0,8},{2,10},{4,12},{6,14},{9,1},{11,3}... | collective-permute-start | bytes 393224 | tf_op jit(solution)/shard_map/ppermute | solution.py:17
  126.8 17.0 %collective-permute-start.6 = (bf16[256,4,128]{0,2,1:T(8,128)(2,1)S(1)}, bf16[256,4,128]{0,2,1:T(8,128)(2,1)S(1)}, u32[]{:S(2)}, u32[]{:S(2)}) collective-permute-start(bf16[256,4,128]{0,2,1:T(8,128)(2,1)S(1)} %collective-permute-done.5), channel_id=1, source_target_pairs={{0,2},{2,4},{4,6},{6,8},{8,10},{10,12},{12,14},{14,0},{1,3},{3,5},... | collective-permute-start | bytes 786440 | tf_op jit(solution)/shard_map/ppermute | solution.py:93
  152.0 9.1 %copy-start.3 = (bf16[256,4,128]{2,0,1:T(8,128)(2,1)S(1)}, bf16[256,4,128]{2,0,1:T(8,128)(2,1)}, u32[]{:S(2)}) copy-start(bf16[256,4,128]{2,0,1:T(8,128)(2,1)} %copy.29) | copy-start | bytes 786436
  152.0 9.1 %copy-start.17 = (s32[4]{0:T(128)S(1)}, s32[4]{0:T(128)}, u32[]{:S(2)}) copy-start(s32[4]{0:T(128)} %iota_multiply_fusion) | copy-start | bytes 52
  161.1 28.8 %copy-start.11 = (f32[512]{0:T(512)S(1)}, f32[512]{0:T(512)}, u32[]{:S(2)}) copy-start(f32[512]{0:T(512)} %param.26) | copy-start | bytes 6148
  161.1 28.8 %copy-start.12 = (f32[512]{0:T(512)S(1)}, f32[512]{0:T(512)}, u32[]{:S(2)}) copy-start(f32[512]{0:T(512)} %param.25) | copy-start | bytes 6148
Sparse Core Ops, SparseCore 0:
  8.9 11.7 all-gather.2
  39.4 76.1 all-gather.4
  192.3 7.8 reduce-scatter.1
